TPU v7x, 32 devices: a whole 2x2x4 slice. The times are simulated.
32 devices in a mesh: seq: 8 (over z, x), tp: 4 (over y, core).
Axes of the slice: x: 2, y: 2, z: 4, core: 2. Of those that a mesh axis runs over, the one named last changes fastest.
Arguments:
- hidden_new: bfloat16 [3, 16, 8192], P(None, None, 'seq'), may hold values from -6 to 6
- w_kv: bfloat16 [8192, 8, 256], P('seq', 'tp'), may hold values from -0.0625 to 0.0625
- w_out: bfloat16 [8192, 8192], P('tp', 'seq'), may hold values from -0.0625 to 0.0625
- queries_draft: bfloat16 [3, 4, 8, 32, 128], P(None, None, 'tp'), may hold values from -48 to 48
- queries_verify: bfloat16 [3, 4, 8, 32, 128], P(None, None, 'tp'), may hold values from -48 to 48
- keys_cache: bfloat16 [4, 8, 16384, 128], P(None, 'tp', 'seq'), may hold values from -6 to 6
- values_cache: bfloat16 [4, 8, 16384, 128], P(None, 'tp', 'seq'), may hold values from -6 to 6
- key_levels: bfloat16 [4, 8, 16384, 128], P(None, 'tp', 'seq'), may hold values from -8 to 7, as said below
- value_levels: bfloat16 [4, 8, 16384, 128], P(None, 'tp', 'seq'), may hold values from -8 to 7, as said below
- key_scales: float32 [4, 8, 16384], P(None, 'tp', 'seq'), may hold values from 0.05 to 0.5
- value_scales: float32 [4, 8, 16384], P(None, 'tp', 'seq'), may hold values from 0.1 to 0.4
- lengths: int32 [4], replicated, may hold values from 2 to 16376, as said below
- accepted: int32 [2, 4], replicated, may hold values from 0 to 4, as said below
Outputs:
- layer_out: bfloat16 [3, 2, 16, 8192], P(None, None, None, 'seq')
Inputs may be any that keep to these rules, and one draw needn't show every extreme that they name: `key_levels`: every entry is a whole number. Positions 0 and 1 of every sequence and head hold equal levels. `value_levels`: every entry is a whole number. `lengths`: some sequence starts with exactly 16376 valid positions, another with 16 or fewer. `accepted`: the values 0 and 4 both occur.
All inputs are finite; a program needn't handle non-finite values.
Results may differ from a plain program's by a relative error of at most 0.006.
The roundings to bfloat16 on the way count: a program that leaves them out, or rounds other values in their place, can miss the bound.
Values may be sent and summed in bfloat16 or wider, within the bound.
A program may use at most 128 MiB of HBM per device.

v0:
```python
import math
import jax
import jax.numpy as jnp
from jax import lax
from jax.sharding import PartitionSpec as P

HD = 128
GROUP = 8
R = 4
ROUNDS = 3
NEG = -1e30


def dequantize(levels, scales):
    return (levels.astype(jnp.float32) * scales[..., None]).astype(jnp.bfloat16)


def attend(queries, keys, values, usable):
    scores = jnp.einsum("bhqd,bhkd->bhqk", queries, keys, preferred_element_type=jnp.float32) * (
        1.0 / math.sqrt(HD)
    )
    scores = jnp.where(usable, scores, NEG)
    maxima = jnp.max(scores, axis=-1)
    weights = jnp.where(usable, jnp.exp(scores - maxima[..., None]), 0.0).astype(jnp.bfloat16)
    totals = jnp.sum(weights.astype(jnp.float32), axis=-1)
    weighted = jnp.einsum("bhqk,bhkd->bhqd", weights, values, preferred_element_type=jnp.float32)
    return (maxima, totals, weighted)


def combine(former, latter):
    highest = jnp.maximum(former[0], latter[0])
    former_w = jnp.exp(former[0] - highest)
    latter_w = jnp.exp(latter[0] - highest)
    return (
        highest,
        former[1] * former_w + latter[1] * latter_w,
        former[2] * former_w[..., None] + latter[2] * latter_w[..., None],
    )


def finish(partial_value):
    return (partial_value[2] / partial_value[1][..., None]).astype(jnp.bfloat16)


def arrange(attended):
    kind_count, batch_size, head_count, query_rows, head_width = attended.shape
    split_rows = attended.reshape(kind_count, batch_size, head_count, GROUP, R, head_width)
    return split_rows.transpose(0, 1, 4, 2, 3, 5).reshape(
        kind_count * batch_size * R, head_count * GROUP * head_width
    )


def stacked_rows(draft_part, verify_part):
    maxima = jnp.stack([draft_part[0], verify_part[0]]).reshape(1, -1)
    totals = jnp.stack([draft_part[1], verify_part[1]]).reshape(1, -1)
    weighted = jnp.stack([draft_part[2], verify_part[2]]).reshape(1, maxima.shape[1], -1)
    return (maxima, totals, weighted)


def spread_merge(draft_part, verify_part, draft_self, verify_self, seq_index):
    maxima, totals, weighted = stacked_rows(draft_part, verify_part)
    maxima, totals, weighted = (
        lax.all_to_all(maxima, "seq", split_axis=1, concat_axis=0, tiled=True),
        lax.all_to_all(totals, "seq", split_axis=1, concat_axis=0, tiled=True),
        lax.all_to_all(weighted, "seq", split_axis=1, concat_axis=0, tiled=True),
    )
    highest = jnp.max(maxima, axis=0)
    factors = jnp.exp(maxima - highest[None])
    share_part = (
        highest,
        jnp.sum(totals * factors, axis=0),
        jnp.sum(weighted * factors[..., None], axis=0),
    )
    share_rows = highest.shape[0]
    self_max, self_tot, self_sum = stacked_rows(draft_self, verify_self)
    row_start = seq_index * share_rows
    self_share = (
        lax.dynamic_slice_in_dim(self_max[0], row_start, share_rows, 0),
        lax.dynamic_slice_in_dim(self_tot[0], row_start, share_rows, 0),
        lax.dynamic_slice_in_dim(self_sum[0], row_start, share_rows, 0),
    )
    merged = finish(combine(share_part, self_share))
    gathered = lax.all_gather(merged, "seq", axis=0, tiled=True)
    return gathered.reshape((2,) + draft_part[2].shape)


def per_device(
    hidden_new,
    w_kv,
    w_out,
    queries_draft,
    queries_verify,
    keys_cache,
    values_cache,
    key_levels,
    value_levels,
    key_scales,
    value_scales,
    lengths,
    accepted,
):
    batch_size, head_count, local_len, head_width = keys_cache.shape
    seq_index = lax.axis_index("seq")
    first_row = seq_index * local_len
    key_low = dequantize(key_levels, key_scales)
    value_low = dequantize(value_levels, value_scales)
    places = first_row + jnp.arange(local_len, dtype=jnp.int32)
    stored = (places[None, :] < lengths[:, None])[:, None, :, None]
    flat_kv = w_kv.reshape(w_kv.shape[0], -1)
    tokens = jnp.arange(GROUP * R, dtype=jnp.int32) % R
    causal = (tokens[:, None] >= jnp.arange(R, dtype=jnp.int32)[None, :])[None, None]
    offsets = jnp.arange(R, dtype=jnp.int32)[None, :]
    batch_rows = jnp.broadcast_to(jnp.arange(batch_size, dtype=jnp.int32)[:, None], (batch_size, R))
    length_now = lengths
    results = []
    for turn_index in range(ROUNDS):
        partial_kv = jnp.dot(hidden_new[turn_index], flat_kv, preferred_element_type=jnp.float32)
        fresh_rows = (
            lax.psum(partial_kv, "seq")
            .astype(jnp.bfloat16)
            .reshape(batch_size, R, head_count, 2, head_width)
        )
        new_keys = fresh_rows[:, :, :, 0].transpose(0, 2, 1, 3)
        new_values = fresh_rows[:, :, :, 1].transpose(0, 2, 1, 3)
        usable = (places[None, :] < length_now[:, None])[:, None, None, :]
        draft_q = queries_draft[turn_index]
        verify_q = queries_verify[turn_index]
        draft_keys = jnp.where(stored, key_low, keys_cache)
        draft_values = jnp.where(stored, value_low, values_cache)
        draft_part = attend(draft_q, draft_keys, draft_values, usable)
        draft_self = attend(draft_q, new_keys, new_values, causal)
        verify_part = attend(verify_q, keys_cache, values_cache, usable)
        verify_self = attend(verify_q, new_keys, new_values, causal)
        attended = spread_merge(draft_part, verify_part, draft_self, verify_self, seq_index)
        projected = jnp.dot(arrange(attended), w_out, preferred_element_type=jnp.float32)
        summed = lax.psum(projected, "tp")
        results.append(summed.astype(jnp.bfloat16).reshape(2, batch_size * R, -1))
        if turn_index + 1 < ROUNDS:
            accepted_now = accepted[turn_index]
            targets = length_now[:, None] + offsets - first_row
            landing = (offsets < accepted_now[:, None]) & (targets >= 0) & (targets < local_len)
            targets = jnp.where(landing, targets, local_len)
            keys_cache = keys_cache.at[batch_rows, :, targets, :].set(
                fresh_rows[:, :, :, 0], mode="drop"
            )
            values_cache = values_cache.at[batch_rows, :, targets, :].set(
                fresh_rows[:, :, :, 1], mode="drop"
            )
            length_now = length_now + accepted_now
    return jnp.stack(results)


def solution(mesh):
    return jax.shard_map(
        per_device,
        mesh=mesh,
        in_specs=(
            P(None, None, "seq"),
            P("seq", "tp", None),
            P("tp", "seq"),
            P(None, None, "tp", None, None),
            P(None, None, "tp", None, None),
            P(None, "tp", "seq", None),
            P(None, "tp", "seq", None),
            P(None, "tp", "seq", None),
            P(None, "tp", "seq", None),
            P(None, "tp", "seq"),
            P(None, "tp", "seq"),
            P(),
            P(),
        ),
        out_specs=P(None, None, None, "seq"),
        check_vma=False,
    )
```

profile of v0, /device:TPU:0, one launch (start us, length us, event | category | flops | bytes accessed | tf_op | source)
XLA Modules:
  0.0 335.9 jit_solution(9079900889281217494)
XLA Ops:
  0.0 4.6 %copy.174 = bf16[4,2,2048,128]{3,2,1,0:T(8,128)(2,1)} copy(bf16[4,2,2048,128]{3,2,1,0:T(8,128)(2,1)} %param.18) | data formatting | bytes 8388608
  4.6 2.0 copy.175
  6.7 3.9 %fusion.169 = (f32[4,2,32]{2,1,0:T(2,128)S(1)}, f32[4,2,32,2048]{3,2,1,0:T(8,128)S(1)}) fusion(bf16[4,2,2048,128]{3,2,1,0:T(8,128)(2,1)} %copy.174, bf16[3,4,2,32,128]{4,3,2,1,0:T(8,128)(2,1)S(1)} %copy-done.16, pred[4,2048]{1,0:T(4,128)(4,1)S(1)} %get-tuple-element.48), kind=kOutput, calls=%fused_computation.242 | convolution fusion | flops 135790336 | bytes 6366208 | tf_op jit(solution)/shard_map/bhqd,bhkd->bhqk/dot_general | solution.py:19
  10.7 5.9 %fusion.170 = (f32[4,2,32]{2,1,0:T(2,128)S(1)}, f32[4,2,32,2048]{3,2,1,0:T(8,128)S(1)}) fusion(bf16[3,4,2,32,128]{4,3,2,1,0:T(8,128)(2,1)} %param.16, bf16[4,2,2048,128]{3,2,1,0:T(8,128)(2,1)S(1)} %copy-done.2, pred[4,2048]{1,0:T(4,128)(4,1)S(1)} %get-tuple-element.48, f32[4,2,2048]{2,1,0:T(2,128)S(1)} %copy-done.22, bf16[4,2,2048,128]{3,2,1,0:T(8,128)(2,1)} %param.20), kind=kOutput, calls=%fused_computation.243 | convolution fusion | flops 144178944 | bytes 10634240 | tf_op jit(solution)/shard_map/bhqd,bhkd->bhqk/dot_general | solution.py:19
  16.6 0.9 convert_reduce_fusion.5
  18.6 7.3 %all-to-all-start.2 = ((f32[1,8,64]{2,0,1:T(1,128)}), f32[1,8,64]{2,0,1:T(1,128)S(1)}, u32[]{:S(2)}, u32[]{:S(2)}) async-start(f32[1,8,64]{2,0,1:T(1,128)} %all_to_all.104), calls=%async_computation.2 | async-start | bytes 8192 | tf_op jit(solution)/shard_map/all_to_all | solution.py:64
  26.9 38.5 %all-reduce = (bf16[16,512]{1,0:T(8,128)(2,1)S(1)}, bf16[16,512]{1,0:T(8,128)(2,1)S(1)}, bf16[16,512]{1,0:T(8,128)(2,1)S(1)}) all-reduce(f32[16,512]{1,0:T(8,128)S(1)} %fusion.111, f32[16,512]{1,0:T(8,128)S(1)} %fusion.115, f32[16,512]{1,0:T(8,128)S(1)} %fusion.113), channel_id=1, replica_groups=mesh['seq'=8,'tp'=4] {'seq'}, use_global_device_ids=true, to_apply=%region_34.35 | all-reduce | flops 24576 | bytes 147456 | tf_op jit(solution)/shard_map/psum | solution.py:119
  66.8 2.5 scatter_fusion
  69.3 10.5 %copy.76 = bf16[4,2,2048,128]{3,1,2,0:T(2,128)(2,1)} copy(bf16[4,2,2048,128]{3,2,1,0:T(8,128)(2,1)} %scatter_fusion) | data formatting | bytes 8388608 | tf_op jit(solution)/shard_map/scatter | solution.py:143
  80.0 2.6 scatter_fusion.2
  82.6 8.5 %fusion.162 = (f32[4,2,32]{2,1,0:T(2,128)S(1)}, f32[4,2,32,2048]{3,2,1,0:T(8,128)}) fusion(bf16[3,4,2,32,128]{4,3,2,1,0:T(8,128)(2,1)S(1)} %copy-done.21, pred[4,2048]{1,0:T(4,128)(4,1)S(1)} %get-tuple-element.48, bf16[4,2,2048,128]{3,1,2,0:T(2,128)(2,1)} %scatter_fusion.2, f32[4,2,2048]{2,1,0:T(2,128)S(1)} %copy-done.23, ...), kind=kOutput, calls=%fused_computation.235 | convolution fusion | flops 144178944 | bytes 10634240 | tf_op jit(solution)/shard_map/bhqd,bhkd->bhqk/dot_general | solution.py:19
  91.1 2.9 fusion.161
  94.0 6.2 %fusion.168 = (f32[4,2,32]{2,1,0:T(2,128)S(1)}, f32[4,2,32,2048]{3,2,1,0:T(8,128)}) fusion(bf16[3,4,2,32,128]{4,3,2,1,0:T(8,128)(2,1)S(1)} %copy-done.21, bf16[4,2,2048,128]{3,2,1,0:T(8,128)(2,1)S(1)} %copy-done.3, pred[4,2048]{1,0:T(4,128)(4,1)S(1)} %get-tuple-element.48, f32[4,2,2048]{2,1,0:T(2,128)S(1)} %copy-done.23, ...), kind=kOutput, calls=%fused_computation.241 | convolution fusion | flops 144178944 | bytes 10634240 | tf_op jit(solution)/shard_map/bhqd,bhkd->bhqk/dot_general | solution.py:19
  100.2 2.8 fusion.167
  103.1 0.9 convolution_bitcast_fusion.1
  104.7 1.2 copy-done.20
  105.9 4.2 %fusion.66 = f32[1,4,2,32,128]{4,3,2,1,0:T(8,128)S(1)} fusion(bf16[4,2,2048,128]{3,2,1,0:T(8,128)(2,1)S(1)} %copy-done, pred[4,2048]{1,0:T(4,128)(4,1)S(1)} %get-tuple-element.48, f32[4,2,2048]{2,1,0:T(2,128)S(1)} %copy-done.24, bf16[4,2,2048,128]{3,2,1,0:T(8,128)(2,1)S(1)} %copy-done.20, f32[4,2,32,2048]{3,2,1,0:T(8,128)S(1)} %copy-done.9, ...), kind=kOutput, calls=%fused_computation.62 | convolution fusion | flops 144179200 | bytes 10691584 | tf_op jit(solution)/shard_map/bhqk,bhkd->bhqd/dot_general | solution.py:26
  110.9 2.5 scatter_fusion.1
  113.4 10.6 %copy.80 = bf16[4,2,2048,128]{3,1,2,0:T(2,128)(2,1)} copy(bf16[4,2,2048,128]{3,2,1,0:T(8,128)(2,1)} %scatter_fusion.1) | data formatting | bytes 8388608 | tf_op jit(solution)/shard_map/scatter | solution.py:146
  124.0 6.0 %fusion.69 = f32[1,4,2,32,128]{4,3,2,1,0:T(8,128)S(1)} fusion(bf16[4,2,2048,128]{3,2,1,0:T(8,128)(2,1)S(1)} %copy-done.1, pred[4,2048]{1,0:T(4,128)(4,1)S(1)} %get-tuple-element.48, f32[4,2,2048]{2,1,0:T(2,128)S(1)} %copy-done.24, bf16[4,2,2048,128]{3,2,1,0:T(8,128)(2,1)} %param.21, f32[4,2,32,2048]{3,2,1,0:T(8,128)S(1)} %copy-done.12, ...), kind=kOutput, calls=%fused_computation.63 | convolution fusion | flops 144179200 | bytes 10699776 | tf_op jit(solution)/shard_map/bhqk,bhkd->bhqd/dot_general | solution.py:26
  130.0 0.9 convolution_bitcast_fusion
  131.0 2.6 scatter_fusion.3
  133.6 7.2 %fusion.72 = f32[1,4,2,32,128]{4,3,2,1,0:T(8,128)S(1)} fusion(pred[4,2048]{1,0:T(4,128)(4,1)S(1)} %get-tuple-element.48, bf16[4,2,2048,128]{3,1,2,0:T(2,128)(2,1)} %scatter_fusion.3, f32[4,2,2048]{2,1,0:T(2,128)S(1)} %copy-done.24, bf16[4,2,2048,128]{3,2,1,0:T(8,128)(2,1)} %param.21, f32[4,2,32,2048]{3,2,1,0:T(8,128)} %get-tuple-element.58, ...), kind=kOutput, calls=%fused_computation.64 | convolution fusion | flops 144179200 | bytes 10699776 | tf_op jit(solution)/shard_map/bhqk,bhkd->bhqd/dot_general | solution.py:26
  140.8 1.9 convert_reduce_fusion.1
  143.0 1.0 fusion.63
  145.6 0.7 pad_maximum_fusion.2
  146.3 0.7 pad_maximum_fusion.4
  147.8 3.2 all-to-all-start.1
  151.7 5.7 %all-to-all-done.1 = f32[1,8,64]{2,0,1:T(1,128)S(1)} async-done(((f32[1,8,64]{2,0,1:T(1,128)}), f32[1,8,64]{2,0,1:T(1,128)S(1)}, u32[]{:S(2)}, u32[]{:S(2)}) %all-to-all-start.1) | async-done | bytes 2080 | tf_op jit(solution)/shard_map/all_to_all | solution.py:63
  157.4 3.3 all-to-all-start.4
  163.4 3.8 %all-to-all-done.4 = f32[1,8,64]{2,0,1:T(1,128)S(1)} async-done(((f32[1,8,64]{2,0,1:T(1,128)}), f32[1,8,64]{2,0,1:T(1,128)S(1)}, u32[]{:S(2)}, u32[]{:S(2)}) %all-to-all-start.4) | async-done | bytes 2080 | tf_op jit(solution)/shard_map/all_to_all | solution.py:63
  167.2 3.3 all-to-all-start.5
  170.5 6.4 %all-to-all-done.5 = f32[1,8,64]{2,0,1:T(1,128)S(1)} async-done(((f32[1,8,64]{2,0,1:T(1,128)}), f32[1,8,64]{2,0,1:T(1,128)S(1)}, u32[]{:S(2)}, u32[]{:S(2)}) %all-to-all-start.5) | async-done | bytes 2080 | tf_op jit(solution)/shard_map/all_to_all | solution.py:64
  176.9 3.3 all-to-all-start.8
  180.3 6.3 %all-to-all-done.8 = f32[1,8,64]{2,0,1:T(1,128)S(1)} async-done(((f32[1,8,64]{2,0,1:T(1,128)}), f32[1,8,64]{2,0,1:T(1,128)S(1)}, u32[]{:S(2)}, u32[]{:S(2)}) %all-to-all-start.8) | async-done | bytes 2080 | tf_op jit(solution)/shard_map/all_to_all | solution.py:64
  186.6 3.2 all-to-all-start.7
  189.9 6.3 %all-to-all-done.7 = f32[1,8,64]{2,0,1:T(1,128)S(1)} async-done(((f32[1,8,64]{2,0,1:T(1,128)}), f32[1,8,64]{2,0,1:T(1,128)S(1)}, u32[]{:S(2)}, u32[]{:S(2)}) %all-to-all-start.7) | async-done | bytes 2080 | tf_op jit(solution)/shard_map/all_to_all | solution.py:63
  196.2 3.4 %all-to-all-start = ((f32[1,512,128]{2,0,1:T(1,128)}), f32[1,512,128]{2,0,1:T(1,128)S(1)}, u32[]{:S(2)}, u32[]{:S(2)}) async-start(f32[1,512,128]{2,0,1:T(1,128)} %bitcast.6), calls=%async_computation | async-start | bytes 524288 | tf_op jit(solution)/shard_map/all_to_all | solution.py:65
  199.9 7.9 %all-to-all-done = f32[1,512,128]{2,0,1:T(1,128)S(1)} async-done(((f32[1,512,128]{2,0,1:T(1,128)}), f32[1,512,128]{2,0,1:T(1,128)S(1)}, u32[]{:S(2)}, u32[]{:S(2)}) %all-to-all-start) | async-done | bytes 262176 | tf_op jit(solution)/shard_map/all_to_all | solution.py:65
  207.8 3.4 %all-to-all-start.3 = ((f32[1,512,128]{2,0,1:T(1,128)}), f32[1,512,128]{2,0,1:T(1,128)S(1)}, u32[]{:S(2)}, u32[]{:S(2)}) async-start(f32[1,512,128]{2,0,1:T(1,128)} %bitcast.43), calls=%async_computation.3 | async-start | bytes 524288 | tf_op jit(solution)/shard_map/all_to_all | solution.py:65
  211.5 32.1 %all_gather.9 = bf16[512,128]{1,0:T(8,128)(2,1)S(1)} all-gather(bf16[64,128]{1,0:T(8,128)(2,1)S(1)} %divide_convert_fusion.2), channel_id=1, replica_groups=mesh['seq'=8,'tp'=4] {'seq'}, dimensions={0}, use_global_device_ids=true | all-gather | bytes 147456 | tf_op jit(solution)/shard_map/all_gather | solution.py:83
  243.7 3.0 fusion.171
  246.7 4.5 %all-to-all-start.6 = ((f32[1,512,128]{2,0,1:T(1,128)}), f32[1,512,128]{2,0,1:T(1,128)S(1)}, u32[]{:S(2)}, u32[]{:S(2)}) async-start(f32[1,512,128]{2,0,1:T(1,128)} %bitcast.80), calls=%async_computation.6 | async-start | bytes 524288 | tf_op jit(solution)/shard_map/all_to_all | solution.py:65
  251.5 32.0 %all_gather.10 = bf16[512,128]{1,0:T(8,128)(2,1)S(1)} all-gather(bf16[64,128]{1,0:T(8,128)(2,1)S(1)} %divide_convert_fusion.1), channel_id=1, replica_groups=mesh['seq'=8,'tp'=4] {'seq'}, dimensions={0}, use_global_device_ids=true | all-gather | bytes 147456 | tf_op jit(solution)/shard_map/all_gather | solution.py:83
  283.5 3.0 fusion.172
  286.8 30.5 %all_gather.11 = bf16[512,128]{1,0:T(8,128)(2,1)S(1)} all-gather(bf16[64,128]{1,0:T(8,128)(2,1)S(1)} %divide_convert_fusion), channel_id=1, replica_groups=mesh['seq'=8,'tp'=4] {'seq'}, dimensions={0}, use_global_device_ids=true | all-gather | bytes 147456 | tf_op jit(solution)/shard_map/all_gather | solution.py:83
  317.4 3.0 fusion.173
  320.4 14.8 %all-reduce.3 = (bf16[32,1024]{1,0:T(8,128)(2,1)S(1)}, bf16[32,1024]{1,0:T(8,128)(2,1)S(1)}, bf16[32,1024]{1,0:T(8,128)(2,1)S(1)}) all-reduce(f32[32,1024]{1,0:T(8,128)S(1)} %fusion.173, f32[32,1024]{1,0:T(8,128)S(1)} %fusion.172, f32[32,1024]{1,0:T(8,128)S(1)} %fusion.171), channel_id=1, replica_groups=mesh['seq'=8,'tp'=4] {'tp'}, use_global_device_ids=true, to_apply=%region_42.43 | all-reduce | flops 98304 | bytes 589824 | tf_op jit(solution)/shard_map/psum | solution.py:136
  (141 shorter events, 12.9 us)
Async XLA Ops:
  0.0 4.6 %copy-start.7 = (bf16[4,2,2048,128]{3,2,1,0:T(8,128)(2,1)S(1)}, bf16[4,2,2048,128]{3,2,1,0:T(8,128)(2,1)}, u32[]{:S(2)}) copy-start(bf16[4,2,2048,128]{3,2,1,0:T(8,128)(2,1)} %param.19) | copy-start | bytes 12582916
  4.6 2.0 copy-start.17
  4.6 2.0 copy-start.18
  4.6 2.1 copy-start.16
  6.7 4.0 %copy-start.2 = (bf16[4,2,2048,128]{3,2,1,0:T(8,128)(2,1)S(1)}, bf16[4,2,2048,128]{3,2,1,0:T(8,128)(2,1)}, u32[]{:S(2)}) copy-start(bf16[4,2,2048,128]{3,2,1,0:T(8,128)(2,1)} %copy.174) | copy-start | bytes 12582916
  6.7 4.0 %copy-start.22 = (f32[4,2,2048]{2,1,0:T(2,128)S(1)}, f32[4,2,2048]{2,1,0:T(2,128)}, u32[]{:S(2)}) copy-start(f32[4,2,2048]{2,1,0:T(2,128)} %param.22) | copy-start | bytes 196612
  16.6 1.3 copy-start.8
  16.6 9.3 %copy-start.14 = (bf16[1024,2,256]{2,1,0:T(2,128)(2,1)S(1)}, bf16[1024,2,256]{2,1,0:T(2,128)(2,1)}, u32[]{:S(2)}) copy-start(bf16[1024,2,256]{2,1,0:T(2,128)(2,1)} %param.14) | copy-start | bytes 3145732
  17.9 8.2 %copy-start.15 = (bf16[3,16,1024]{2,1,0:T(8,128)(2,1)S(1)}, bf16[3,16,1024]{2,1,0:T(8,128)(2,1)}, u32[]{:S(2)}) copy-start(bf16[3,16,1024]{2,1,0:T(8,128)(2,1)} %param.13) | copy-start | bytes 294916
  18.6 129.2 %all-to-all-start.2 = ((f32[1,8,64]{2,0,1:T(1,128)}), f32[1,8,64]{2,0,1:T(1,128)S(1)}, u32[]{:S(2)}, u32[]{:S(2)}) async-start(f32[1,8,64]{2,0,1:T(1,128)} %all_to_all.104), calls=%async_computation.2 | async-start | bytes 8192 | tf_op jit(solution)/shard_map/all_to_all | solution.py:64
  26.1 39.5 %copy-start.21 = (bf16[3,4,2,32,128]{4,3,2,1,0:T(8,128)(2,1)S(1)}, bf16[3,4,2,32,128]{4,3,2,1,0:T(8,128)(2,1)}, u32[]{:S(2)}) copy-start(bf16[3,4,2,32,128]{4,3,2,1,0:T(8,128)(2,1)} %param.16) | copy-start | bytes 589828
  69.3 13.3 %copy-start.23 = (f32[4,2,2048]{2,1,0:T(2,128)S(1)}, f32[4,2,2048]{2,1,0:T(2,128)}, u32[]{:S(2)}) copy-start(f32[4,2,2048]{2,1,0:T(2,128)} %param.22) | copy-start | bytes 196612
  82.6 8.5 %copy-start.6 = (bf16[4,2,2048,128]{3,1,2,0:T(2,128)(2,1)S(1)}, bf16[4,2,2048,128]{3,1,2,0:T(2,128)(2,1)}, u32[]{:S(2)}) copy-start(bf16[4,2,2048,128]{3,1,2,0:T(2,128)(2,1)} %scatter_fusion.2) | copy-start | bytes 12582916
  82.6 11.4 %copy-start.19 = (bf16[4,2,2048,128]{3,2,1,0:T(8,128)(2,1)S(1)}, bf16[4,2,2048,128]{3,2,1,0:T(8,128)(2,1)}, u32[]{:S(2)}) copy-start(bf16[4,2,2048,128]{3,2,1,0:T(8,128)(2,1)} %param.20) | copy-start | bytes 12582916
  91.1 2.9 copy-start.3
  100.2 2.8 copy-start
  103.1 1.6 copy-start.9
  103.1 2.8 copy-start.20
  103.1 2.8 copy-start.24
  113.4 10.6 %copy-start.1 = (bf16[4,2,2048,128]{3,2,1,0:T(8,128)(2,1)S(1)}, bf16[4,2,2048,128]{3,2,1,0:T(8,128)(2,1)}, u32[]{:S(2)}) copy-start(bf16[4,2,2048,128]{3,2,1,0:T(8,128)(2,1)} %scatter_fusion.1) | copy-start | bytes 12582916
  113.4 10.6 %copy-start.12 = (f32[4,2,32,2048]{3,2,1,0:T(8,128)S(1)}, f32[4,2,32,2048]{3,2,1,0:T(8,128)}, u32[]{:S(2)}) copy-start(f32[4,2,32,2048]{3,2,1,0:T(8,128)} %get-tuple-element.70) | copy-start | bytes 6291460
  124.0 6.0 %copy-start.4 = (f32[4,2,32,2048]{3,2,1,0:T(8,128)S(1)}, f32[4,2,32,2048]{3,2,1,0:T(8,128)}, u32[]{:S(2)}) copy-start(f32[4,2,32,2048]{3,2,1,0:T(8,128)} %get-tuple-element.68) | copy-start | bytes 6291460
  133.6 7.2 %copy-start.10 = (f32[4,2,32,2048]{3,2,1,0:T(8,128)S(1)}, f32[4,2,32,2048]{3,2,1,0:T(8,128)}, u32[]{:S(2)}) copy-start(f32[4,2,32,2048]{3,2,1,0:T(8,128)} %get-tuple-element.56) | copy-start | bytes 6291460
  133.6 7.2 %copy-start.11 = (f32[4,2,32,2048]{3,2,1,0:T(8,128)S(1)}, f32[4,2,32,2048]{3,2,1,0:T(8,128)}, u32[]{:S(2)}) copy-start(f32[4,2,32,2048]{3,2,1,0:T(8,128)} %get-tuple-element.58) | copy-start | bytes 6291460
  133.6 7.2 %copy-start.13 = (f32[4,2,32,2048]{3,2,1,0:T(8,128)S(1)}, f32[4,2,32,2048]{3,2,1,0:T(8,128)}, u32[]{:S(2)}) copy-start(f32[4,2,32,2048]{3,2,1,0:T(8,128)} %get-tuple-element.70) | copy-start | bytes 6291460
  140.8 2.2 copy-start.5
  147.8 9.7 %all-to-all-start.1 = ((f32[1,8,64]{2,0,1:T(1,128)}), f32[1,8,64]{2,0,1:T(1,128)S(1)}, u32[]{:S(2)}, u32[]{:S(2)}) async-start(f32[1,8,64]{2,0,1:T(1,128)} %all_to_all.101), calls=%async_computation.1 | async-start | bytes 8192 | tf_op jit(solution)/shard_map/all_to_all | solution.py:63
  157.4 9.8 %all-to-all-start.4 = ((f32[1,8,64]{2,0,1:T(1,128)}), f32[1,8,64]{2,0,1:T(1,128)S(1)}, u32[]{:S(2)}, u32[]{:S(2)}) async-start(f32[1,8,64]{2,0,1:T(1,128)} %all_to_all.109), calls=%async_computation.4 | async-start | bytes 8192 | tf_op jit(solution)/shard_map/all_to_all | solution.py:63
  167.2 9.7 %all-to-all-start.5 = ((f32[1,8,64]{2,0,1:T(1,128)}), f32[1,8,64]{2,0,1:T(1,128)S(1)}, u32[]{:S(2)}, u32[]{:S(2)}) async-start(f32[1,8,64]{2,0,1:T(1,128)} %all_to_all.112), calls=%async_computation.5 | async-start | bytes 8192 | tf_op jit(solution)/shard_map/all_to_all | solution.py:64
  176.9 9.7 %all-to-all-start.8 = ((f32[1,8,64]{2,0,1:T(1,128)}), f32[1,8,64]{2,0,1:T(1,128)S(1)}, u32[]{:S(2)}, u32[]{:S(2)}) async-start(f32[1,8,64]{2,0,1:T(1,128)} %all_to_all.120), calls=%async_computation.8 | async-start | bytes 8192 | tf_op jit(solution)/shard_map/all_to_all | solution.py:64
  186.6 9.7 %all-to-all-start.7 = ((f32[1,8,64]{2,0,1:T(1,128)}), f32[1,8,64]{2,0,1:T(1,128)S(1)}, u32[]{:S(2)}, u32[]{:S(2)}) async-start(f32[1,8,64]{2,0,1:T(1,128)} %all_to_all.117), calls=%async_computation.7 | async-start | bytes 8192 | tf_op jit(solution)/shard_map/all_to_all | solution.py:63
  196.2 11.6 %all-to-all-start = ((f32[1,512,128]{2,0,1:T(1,128)}), f32[1,512,128]{2,0,1:T(1,128)S(1)}, u32[]{:S(2)}, u32[]{:S(2)}) async-start(f32[1,512,128]{2,0,1:T(1,128)} %bitcast.6), calls=%async_computation | async-start | bytes 524288 | tf_op jit(solution)/shard_map/all_to_all | solution.py:65
  207.8 38.8 %all-to-all-start.3 = ((f32[1,512,128]{2,0,1:T(1,128)}), f32[1,512,128]{2,0,1:T(1,128)S(1)}, u32[]{:S(2)}, u32[]{:S(2)}) async-start(f32[1,512,128]{2,0,1:T(1,128)} %bitcast.43), calls=%async_computation.3 | async-start | bytes 524288 | tf_op jit(solution)/shard_map/all_to_all | solution.py:65
  246.7 39.8 %all-to-all-start.6 = ((f32[1,512,128]{2,0,1:T(1,128)}), f32[1,512,128]{2,0,1:T(1,128)S(1)}, u32[]{:S(2)}, u32[]{:S(2)}) async-start(f32[1,512,128]{2,0,1:T(1,128)} %bitcast.80), calls=%async_computation.6 | async-start | bytes 524288 | tf_op jit(solution)/shard_map/all_to_all | solution.py:65
where the time goes:
time: 337 us; the launch traced here: 336 us
  blocking collectives  148 us (44%)
  matrix products  62.7 us (19%)
  local copies, waits for them, and re-layouts  45.8 us (14%)
  waiting for transfers between devices  36.6 us (11%)
  starting transfers between devices  35 us (10%)
  other arithmetic  7.3 us (2%)
    all_gather x3, blocking collectives, spread_merge(): gathered = lax.all_gather(merged, 'seq', axis=0, tiled=True)  94.5 us
    psum x1, blocking collectives, per_device(): lax.psum(partial_kv, 'seq').astype(jnp.bfloat16)  38.5 us
    dot_general x12, matrix products, attend(): jnp.einsum('bhqd,bhkd->bhqk', queries, keys, preferred_element_type=jnp.f...  31.3 us
    dot_general x12, matrix products, attend(): jnp.einsum('bhqk,bhkd->bhqd', weights, values, preferred_element_type=jnp...  21.6 us
    all_to_all x3, waiting for transfers between devices, spread_merge(): lax.all_to_all(maxima, 'seq', split_axis=1, concat_axis=0, tiled=True)  15.9 us
    scatter x3, local copies, waits for them, and re-layouts, per_device(): values_cache.at[batch_rows, :, targets, :]  15.7 us
    scatter x3, local copies, waits for them, and re-layouts, per_device(): keys_cache.at[batch_rows, :, targets, :]  15.6 us
    psum x1, blocking collectives, per_device(): summed = lax.psum(projected, 'tp')  14.8 us
  transfers between devices with their start and end apart: 9, of which 6 were waited for; matrix products, arithmetic and copies ran while one was open for 26% of the time, Pallas kernels for 0%

commit v1 on v0

--- a/solution.py
+++ b/solution.py
@@ -61,7 +61,10 @@
     maxima, totals, weighted = stacked_rows(draft_part, verify_part)
     maxima, totals, weighted = (
         lax.all_to_all(maxima, "seq", split_axis=1, concat_axis=0, tiled=True),
-        lax.all_to_all(totals, "seq", split_axis=1, concat_axis=0, tiled=True),
+        jnp.concatenate(
+            lax.all_to_all(jnp.stack(jnp.split(totals, lax.axis_size("seq"), axis=1)), "seq", 0, 0),
+            axis=0,
+        ),
         lax.all_to_all(weighted, "seq", split_axis=1, concat_axis=0, tiled=True),
     )
     highest = jnp.max(maxima, axis=0)

time: 337 us -> 351 us (1.042)
  local copies, waits for them, and re-layouts: 45.8 us -> 58 us
    unnamed x53 -> x74, local copies, waits for them, and re-layouts: 9.41 us -> 21.5 us
  transfers between devices with their start and end apart: 9 -> 9, of which waited for: 6 -> 6; matrix products, arithmetic and copies ran while one was open for 26% -> 28% of each run, Pallas kernels for 0% -> 0%
where the time goes in v1:
time: 351 us; the launch traced here: 350 us
  blocking collectives  148 us (42%)
  matrix products  62.8 us (18%)
  local copies, waits for them, and re-layouts  58 us (17%)
  waiting for transfers between devices  38 us (11%)
  starting transfers between devices  35.1 us (10%)
  other arithmetic  7.3 us (2%)
    all_gather x3, blocking collectives, spread_merge(): gathered = lax.all_gather(merged, 'seq', axis=0, tiled=True)  94.6 us
    psum x1, blocking collectives, per_device(): lax.psum(partial_kv, 'seq').astype(jnp.bfloat16)  38.5 us
    dot_general x12, matrix products, attend(): jnp.einsum('bhqd,bhkd->bhqk', queries, keys, preferred_element_type=jnp.f...  31.4 us
    dot_general x12, matrix products, attend(): jnp.einsum('bhqk,bhkd->bhqd', weights, values, preferred_element_type=jnp...  21.6 us
    unnamed x74, local copies, waits for them, and re-layouts  21.5 us
    all_to_all x3, waiting for transfers between devices, spread_merge(): lax.all_to_all(maxima, 'seq', split_axis=1, concat_axis=0, tiled=True)  17.3 us
    scatter x3, local copies, waits for them, and re-layouts, per_device(): values_cache.at[batch_rows, :, targets, :]  15.7 us
    scatter x3, local copies, waits for them, and re-layouts, per_device(): keys_cache.at[batch_rows, :, targets, :]  15.5 us
  transfers between devices with their start and end apart: 9, of which 6 were waited for; matrix products, arithmetic and copies ran while one was open for 28% of the time, Pallas kernels for 0%

profile of v1, /device:TPU:0, one launch (start us, length us, event | category | flops | bytes accessed | tf_op | source)
XLA Modules:
  0.0 349.7 jit_solution(16772266583895240744)
XLA Ops:
  0.0 4.6 %copy.195 = bf16[4,2,2048,128]{3,2,1,0:T(8,128)(2,1)} copy(bf16[4,2,2048,128]{3,2,1,0:T(8,128)(2,1)} %param.18) | data formatting | bytes 8388608
  4.6 1.9 copy.196
  6.7 3.9 %fusion.169 = (f32[4,2,32]{2,1,0:T(2,128)S(1)}, f32[4,2,32,2048]{3,2,1,0:T(8,128)S(1)}) fusion(bf16[4,2,2048,128]{3,2,1,0:T(8,128)(2,1)} %copy.195, bf16[3,4,2,32,128]{4,3,2,1,0:T(8,128)(2,1)S(1)} %copy-done.16, pred[4,2048]{1,0:T(4,128)(4,1)S(1)} %get-tuple-element.48), kind=kOutput, calls=%fused_computation.290 | convolution fusion | flops 135790336 | bytes 6366208 | tf_op jit(solution)/shard_map/bhqd,bhkd->bhqk/dot_general | solution.py:19
  10.7 5.9 %fusion.170 = (f32[4,2,32]{2,1,0:T(2,128)S(1)}, f32[4,2,32,2048]{3,2,1,0:T(8,128)S(1)}) fusion(bf16[3,4,2,32,128]{4,3,2,1,0:T(8,128)(2,1)} %param.16, bf16[4,2,2048,128]{3,2,1,0:T(8,128)(2,1)S(1)} %copy-done.2, pred[4,2048]{1,0:T(4,128)(4,1)S(1)} %get-tuple-element.48, f32[4,2,2048]{2,1,0:T(2,128)S(1)} %copy-done.22, bf16[4,2,2048,128]{3,2,1,0:T(8,128)(2,1)} %param.20), kind=kOutput, calls=%fused_computation.291 | convolution fusion | flops 144178944 | bytes 10634240 | tf_op jit(solution)/shard_map/bhqd,bhkd->bhqk/dot_general | solution.py:19
  16.6 0.9 convert_reduce_fusion.5
  22.8 7.3 %all-to-all-start.2 = ((f32[8,1,64]{2,1,0:T(1,128)}), f32[8,1,64]{2,1,0:T(1,128)S(1)}, u32[]{:S(2)}, u32[]{:S(2)}) async-start(f32[8,1,64]{2,1,0:T(1,128)} %constant_dynamic-update-slice_fusion), calls=%async_computation.2 | async-start | bytes 8192 | tf_op jit(solution)/shard_map/all_to_all | solution.py:65
  31.1 38.5 %all-reduce = (bf16[16,512]{1,0:T(8,128)(2,1)S(1)}, bf16[16,512]{1,0:T(8,128)(2,1)S(1)}, bf16[16,512]{1,0:T(8,128)(2,1)S(1)}) all-reduce(f32[16,512]{1,0:T(8,128)S(1)} %fusion.111, f32[16,512]{1,0:T(8,128)S(1)} %fusion.115, f32[16,512]{1,0:T(8,128)S(1)} %fusion.113), channel_id=1, replica_groups=mesh['seq'=8,'tp'=4] {'seq'}, use_global_device_ids=true, to_apply=%region_34.35 | all-reduce | flops 24576 | bytes 147456 | tf_op jit(solution)/shard_map/psum | solution.py:122
  71.0 2.5 scatter_fusion
  73.5 10.5 %copy.76 = bf16[4,2,2048,128]{3,1,2,0:T(2,128)(2,1)} copy(bf16[4,2,2048,128]{3,2,1,0:T(8,128)(2,1)} %scatter_fusion) | data formatting | bytes 8388608 | tf_op jit(solution)/shard_map/scatter | solution.py:146
  84.2 2.6 scatter_fusion.2
  86.7 8.5 %fusion.162 = (f32[4,2,32]{2,1,0:T(2,128)S(1)}, f32[4,2,32,2048]{3,2,1,0:T(8,128)}) fusion(bf16[3,4,2,32,128]{4,3,2,1,0:T(8,128)(2,1)S(1)} %copy-done.21, pred[4,2048]{1,0:T(4,128)(4,1)S(1)} %get-tuple-element.48, bf16[4,2,2048,128]{3,1,2,0:T(2,128)(2,1)} %scatter_fusion.2, f32[4,2,2048]{2,1,0:T(2,128)S(1)} %copy-done.23, ...), kind=kOutput, calls=%fused_computation.283 | convolution fusion | flops 144178944 | bytes 10634240 | tf_op jit(solution)/shard_map/bhqd,bhkd->bhqk/dot_general | solution.py:19
  95.2 2.9 fusion.161
  98.2 6.2 %fusion.168 = (f32[4,2,32]{2,1,0:T(2,128)S(1)}, f32[4,2,32,2048]{3,2,1,0:T(8,128)}) fusion(bf16[3,4,2,32,128]{4,3,2,1,0:T(8,128)(2,1)S(1)} %copy-done.21, bf16[4,2,2048,128]{3,2,1,0:T(8,128)(2,1)S(1)} %copy-done.3, pred[4,2048]{1,0:T(4,128)(4,1)S(1)} %get-tuple-element.48, f32[4,2,2048]{2,1,0:T(2,128)S(1)} %copy-done.23, ...), kind=kOutput, calls=%fused_computation.289 | convolution fusion | flops 144178944 | bytes 10634240 | tf_op jit(solution)/shard_map/bhqd,bhkd->bhqk/dot_general | solution.py:19
  104.4 2.9 fusion.167
  107.3 0.9 convolution_bitcast_fusion.1
  108.9 1.2 copy-done.20
  110.1 4.2 %fusion.66 = f32[1,4,2,32,128]{4,3,2,1,0:T(8,128)S(1)} fusion(bf16[4,2,2048,128]{3,2,1,0:T(8,128)(2,1)S(1)} %copy-done, pred[4,2048]{1,0:T(4,128)(4,1)S(1)} %get-tuple-element.48, f32[4,2,2048]{2,1,0:T(2,128)S(1)} %copy-done.24, bf16[4,2,2048,128]{3,2,1,0:T(8,128)(2,1)S(1)} %copy-done.20, f32[4,2,32,2048]{3,2,1,0:T(8,128)S(1)} %copy-done.9, ...), kind=kOutput, calls=%fused_computation.62 | convolution fusion | flops 144179200 | bytes 10691584 | tf_op jit(solution)/shard_map/bhqk,bhkd->bhqd/dot_general | solution.py:26
  114.4 0.7 pad_maximum_fusion
  115.1 2.5 scatter_fusion.1
  117.6 10.6 %copy.80 = bf16[4,2,2048,128]{3,1,2,0:T(2,128)(2,1)} copy(bf16[4,2,2048,128]{3,2,1,0:T(8,128)(2,1)} %scatter_fusion.1) | data formatting | bytes 8388608 | tf_op jit(solution)/shard_map/scatter | solution.py:149
  128.2 6.0 %fusion.69 = f32[1,4,2,32,128]{4,3,2,1,0:T(8,128)S(1)} fusion(bf16[4,2,2048,128]{3,2,1,0:T(8,128)(2,1)S(1)} %copy-done.1, pred[4,2048]{1,0:T(4,128)(4,1)S(1)} %get-tuple-element.48, f32[4,2,2048]{2,1,0:T(2,128)S(1)} %copy-done.24, bf16[4,2,2048,128]{3,2,1,0:T(8,128)(2,1)} %param.21, f32[4,2,32,2048]{3,2,1,0:T(8,128)S(1)} %copy-done.12, ...), kind=kOutput, calls=%fused_computation.63 | convolution fusion | flops 144179200 | bytes 10699776 | tf_op jit(solution)/shard_map/bhqk,bhkd->bhqd/dot_general | solution.py:26
  134.3 0.9 convolution_bitcast_fusion
  135.2 2.7 scatter_fusion.3
  137.8 7.2 %fusion.72 = f32[1,4,2,32,128]{4,3,2,1,0:T(8,128)S(1)} fusion(pred[4,2048]{1,0:T(4,128)(4,1)S(1)} %get-tuple-element.48, bf16[4,2,2048,128]{3,1,2,0:T(2,128)(2,1)} %scatter_fusion.3, f32[4,2,2048]{2,1,0:T(2,128)S(1)} %copy-done.24, bf16[4,2,2048,128]{3,2,1,0:T(8,128)(2,1)} %param.21, f32[4,2,32,2048]{3,2,1,0:T(8,128)} %get-tuple-element.58, ...), kind=kOutput, calls=%fused_computation.64 | convolution fusion | flops 144179200 | bytes 10699776 | tf_op jit(solution)/shard_map/bhqk,bhkd->bhqd/dot_general | solution.py:26
  145.1 1.9 convert_reduce_fusion.1
  147.3 1.0 fusion.63
  159.2 0.7 pad_maximum_fusion.2
  161.4 3.3 all-to-all-start.1
  165.4 5.7 %all-to-all-done.1 = f32[1,8,64]{2,0,1:T(1,128)S(1)} async-done(((f32[1,8,64]{2,0,1:T(1,128)}), f32[1,8,64]{2,0,1:T(1,128)S(1)}, u32[]{:S(2)}, u32[]{:S(2)}) %all-to-all-start.1) | async-done | bytes 2080 | tf_op jit(solution)/shard_map/all_to_all | solution.py:63
  171.1 3.2 all-to-all-start.4
  175.6 5.2 %all-to-all-done.4 = f32[1,8,64]{2,0,1:T(1,128)S(1)} async-done(((f32[1,8,64]{2,0,1:T(1,128)}), f32[1,8,64]{2,0,1:T(1,128)S(1)}, u32[]{:S(2)}, u32[]{:S(2)}) %all-to-all-start.4) | async-done | bytes 2080 | tf_op jit(solution)/shard_map/all_to_all | solution.py:63
  180.8 3.3 all-to-all-start.5
  184.2 6.4 %all-to-all-done.5 = f32[8,1,64]{2,1,0:T(1,128)S(1)} async-done(((f32[8,1,64]{2,1,0:T(1,128)}), f32[8,1,64]{2,1,0:T(1,128)S(1)}, u32[]{:S(2)}, u32[]{:S(2)}) %all-to-all-start.5) | async-done | bytes 2080 | tf_op jit(solution)/shard_map/all_to_all | solution.py:65
  190.6 3.3 all-to-all-start.8
  193.9 6.3 %all-to-all-done.8 = f32[8,1,64]{2,1,0:T(1,128)S(1)} async-done(((f32[8,1,64]{2,1,0:T(1,128)}), f32[8,1,64]{2,1,0:T(1,128)S(1)}, u32[]{:S(2)}, u32[]{:S(2)}) %all-to-all-start.8) | async-done | bytes 2080 | tf_op jit(solution)/shard_map/all_to_all | solution.py:65
  200.3 3.3 all-to-all-start.7
  203.7 6.3 %all-to-all-done.7 = f32[1,8,64]{2,0,1:T(1,128)S(1)} async-done(((f32[1,8,64]{2,0,1:T(1,128)}), f32[1,8,64]{2,0,1:T(1,128)S(1)}, u32[]{:S(2)}, u32[]{:S(2)}) %all-to-all-start.7) | async-done | bytes 2080 | tf_op jit(solution)/shard_map/all_to_all | solution.py:63
  210.0 3.4 all-to-all-start
  213.7 8.0 %all-to-all-done = f32[1,512,128]{2,0,1:T(1,128)S(1)} async-done(((f32[1,512,128]{2,0,1:T(1,128)}), f32[1,512,128]{2,0,1:T(1,128)S(1)}, u32[]{:S(2)}, u32[]{:S(2)}) %all-to-all-start) | async-done | bytes 262176 | tf_op jit(solution)/shard_map/all_to_all | solution.py:68
  221.6 3.4 all-to-all-start.3
  225.3 32.1 %all_gather.9 = bf16[512,128]{1,0:T(8,128)(2,1)S(1)} all-gather(bf16[64,128]{1,0:T(8,128)(2,1)S(1)} %divide_convert_fusion.2), channel_id=1, replica_groups=mesh['seq'=8,'tp'=4] {'seq'}, dimensions={0}, use_global_device_ids=true | all-gather | bytes 147456 | tf_op jit(solution)/shard_map/all_gather | solution.py:86
  257.5 3.0 fusion.171
  260.5 4.5 %all-to-all-start.6 = ((f32[1,512,128]{2,0,1:T(1,128)}), f32[1,512,128]{2,0,1:T(1,128)S(1)}, u32[]{:S(2)}, u32[]{:S(2)}) async-start(f32[1,512,128]{2,0,1:T(1,128)} %bitcast.96), calls=%async_computation.6 | async-start | bytes 524288 | tf_op jit(solution)/shard_map/all_to_all | solution.py:68
  265.2 32.0 %all_gather.10 = bf16[512,128]{1,0:T(8,128)(2,1)S(1)} all-gather(bf16[64,128]{1,0:T(8,128)(2,1)S(1)} %divide_convert_fusion.1), channel_id=1, replica_groups=mesh['seq'=8,'tp'=4] {'seq'}, dimensions={0}, use_global_device_ids=true | all-gather | bytes 147456 | tf_op jit(solution)/shard_map/all_gather | solution.py:86
  297.2 3.0 fusion.172
  300.5 30.5 %all_gather.11 = bf16[512,128]{1,0:T(8,128)(2,1)S(1)} all-gather(bf16[64,128]{1,0:T(8,128)(2,1)S(1)} %divide_convert_fusion), channel_id=1, replica_groups=mesh['seq'=8,'tp'=4] {'seq'}, dimensions={0}, use_global_device_ids=true | all-gather | bytes 147456 | tf_op jit(solution)/shard_map/all_gather | solution.py:86
  331.1 3.0 fusion.173
  334.1 14.8 %all-reduce.3 = (bf16[32,1024]{1,0:T(8,128)(2,1)S(1)}, bf16[32,1024]{1,0:T(8,128)(2,1)S(1)}, bf16[32,1024]{1,0:T(8,128)(2,1)S(1)}) all-reduce(f32[32,1024]{1,0:T(8,128)S(1)} %fusion.173, f32[32,1024]{1,0:T(8,128)S(1)} %fusion.172, f32[32,1024]{1,0:T(8,128)S(1)} %fusion.171), channel_id=1, replica_groups=mesh['seq'=8,'tp'=4] {'tp'}, use_global_device_ids=true, to_apply=%region_42.43 | all-reduce | flops 98304 | bytes 589824 | tf_op jit(solution)/shard_map/psum | solution.py:139
  (165 shorter events, 25.1 us)
Async XLA Ops:
  0.0 4.6 %copy-start.7 = (bf16[4,2,2048,128]{3,2,1,0:T(8,128)(2,1)S(1)}, bf16[4,2,2048,128]{3,2,1,0:T(8,128)(2,1)}, u32[]{:S(2)}) copy-start(bf16[4,2,2048,128]{3,2,1,0:T(8,128)(2,1)} %param.19) | copy-start | bytes 12582916
  4.6 1.9 copy-start.17
  4.6 1.9 copy-start.18
  4.6 2.1 copy-start.16
  6.7 4.0 %copy-start.2 = (bf16[4,2,2048,128]{3,2,1,0:T(8,128)(2,1)S(1)}, bf16[4,2,2048,128]{3,2,1,0:T(8,128)(2,1)}, u32[]{:S(2)}) copy-start(bf16[4,2,2048,128]{3,2,1,0:T(8,128)(2,1)} %copy.195) | copy-start | bytes 12582916
  6.7 4.0 %copy-start.22 = (f32[4,2,2048]{2,1,0:T(2,128)S(1)}, f32[4,2,2048]{2,1,0:T(2,128)}, u32[]{:S(2)}) copy-start(f32[4,2,2048]{2,1,0:T(2,128)} %param.22) | copy-start | bytes 196612
  16.6 1.4 copy-start.8
  16.6 13.5 %copy-start.14 = (bf16[1024,2,256]{2,1,0:T(2,128)(2,1)S(1)}, bf16[1024,2,256]{2,1,0:T(2,128)(2,1)}, u32[]{:S(2)}) copy-start(bf16[1024,2,256]{2,1,0:T(2,128)(2,1)} %param.14) | copy-start | bytes 3145732
  18.0 12.4 %copy-start.15 = (bf16[3,16,1024]{2,1,0:T(8,128)(2,1)S(1)}, bf16[3,16,1024]{2,1,0:T(8,128)(2,1)}, u32[]{:S(2)}) copy-start(bf16[3,16,1024]{2,1,0:T(8,128)(2,1)} %param.13) | copy-start | bytes 294916
  22.8 138.6 %all-to-all-start.2 = ((f32[8,1,64]{2,1,0:T(1,128)}), f32[8,1,64]{2,1,0:T(1,128)S(1)}, u32[]{:S(2)}, u32[]{:S(2)}) async-start(f32[8,1,64]{2,1,0:T(1,128)} %constant_dynamic-update-slice_fusion), calls=%async_computation.2 | async-start | bytes 8192 | tf_op jit(solution)/shard_map/all_to_all | solution.py:65
  30.3 39.5 %copy-start.21 = (bf16[3,4,2,32,128]{4,3,2,1,0:T(8,128)(2,1)S(1)}, bf16[3,4,2,32,128]{4,3,2,1,0:T(8,128)(2,1)}, u32[]{:S(2)}) copy-start(bf16[3,4,2,32,128]{4,3,2,1,0:T(8,128)(2,1)} %param.16) | copy-start | bytes 589828
  73.5 13.2 %copy-start.23 = (f32[4,2,2048]{2,1,0:T(2,128)S(1)}, f32[4,2,2048]{2,1,0:T(2,128)}, u32[]{:S(2)}) copy-start(f32[4,2,2048]{2,1,0:T(2,128)} %param.22) | copy-start | bytes 196612
  86.7 8.5 %copy-start.6 = (bf16[4,2,2048,128]{3,1,2,0:T(2,128)(2,1)S(1)}, bf16[4,2,2048,128]{3,1,2,0:T(2,128)(2,1)}, u32[]{:S(2)}) copy-start(bf16[4,2,2048,128]{3,1,2,0:T(2,128)(2,1)} %scatter_fusion.2) | copy-start | bytes 12582916
  86.7 11.4 %copy-start.19 = (bf16[4,2,2048,128]{3,2,1,0:T(8,128)(2,1)S(1)}, bf16[4,2,2048,128]{3,2,1,0:T(8,128)(2,1)}, u32[]{:S(2)}) copy-start(bf16[4,2,2048,128]{3,2,1,0:T(8,128)(2,1)} %param.20) | copy-start | bytes 12582916
  95.2 3.0 copy-start.3
  104.4 2.9 copy-start
  107.3 1.6 copy-start.9
  107.3 2.8 copy-start.20
  107.3 2.8 copy-start.24
  117.6 10.6 %copy-start.1 = (bf16[4,2,2048,128]{3,2,1,0:T(8,128)(2,1)S(1)}, bf16[4,2,2048,128]{3,2,1,0:T(8,128)(2,1)}, u32[]{:S(2)}) copy-start(bf16[4,2,2048,128]{3,2,1,0:T(8,128)(2,1)} %scatter_fusion.1) | copy-start | bytes 12582916
  117.6 10.6 %copy-start.12 = (f32[4,2,32,2048]{3,2,1,0:T(8,128)S(1)}, f32[4,2,32,2048]{3,2,1,0:T(8,128)}, u32[]{:S(2)}) copy-start(f32[4,2,32,2048]{3,2,1,0:T(8,128)} %get-tuple-element.70) | copy-start | bytes 6291460
  128.2 6.0 %copy-start.4 = (f32[4,2,32,2048]{3,2,1,0:T(8,128)S(1)}, f32[4,2,32,2048]{3,2,1,0:T(8,128)}, u32[]{:S(2)}) copy-start(f32[4,2,32,2048]{3,2,1,0:T(8,128)} %get-tuple-element.68) | copy-start | bytes 6291460
  137.8 7.2 %copy-start.10 = (f32[4,2,32,2048]{3,2,1,0:T(8,128)S(1)}, f32[4,2,32,2048]{3,2,1,0:T(8,128)}, u32[]{:S(2)}) copy-start(f32[4,2,32,2048]{3,2,1,0:T(8,128)} %get-tuple-element.56) | copy-start | bytes 6291460
  137.8 7.2 %copy-start.11 = (f32[4,2,32,2048]{3,2,1,0:T(8,128)S(1)}, f32[4,2,32,2048]{3,2,1,0:T(8,128)}, u32[]{:S(2)}) copy-start(f32[4,2,32,2048]{3,2,1,0:T(8,128)} %get-tuple-element.58) | copy-start | bytes 6291460
  137.8 7.2 %copy-start.13 = (f32[4,2,32,2048]{3,2,1,0:T(8,128)S(1)}, f32[4,2,32,2048]{3,2,1,0:T(8,128)}, u32[]{:S(2)}) copy-start(f32[4,2,32,2048]{3,2,1,0:T(8,128)} %get-tuple-element.70) | copy-start | bytes 6291460
  145.1 2.2 copy-start.5
  161.4 9.8 %all-to-all-start.1 = ((f32[1,8,64]{2,0,1:T(1,128)}), f32[1,8,64]{2,0,1:T(1,128)S(1)}, u32[]{:S(2)}, u32[]{:S(2)}) async-start(f32[1,8,64]{2,0,1:T(1,128)} %all_to_all.74), calls=%async_computation.1 | async-start | bytes 8192 | tf_op jit(solution)/shard_map/all_to_all | solution.py:63
  171.1 9.7 %all-to-all-start.4 = ((f32[1,8,64]{2,0,1:T(1,128)}), f32[1,8,64]{2,0,1:T(1,128)S(1)}, u32[]{:S(2)}, u32[]{:S(2)}) async-start(f32[1,8,64]{2,0,1:T(1,128)} %all_to_all.80), calls=%async_computation.4 | async-start | bytes 8192 | tf_op jit(solution)/shard_map/all_to_all | solution.py:63
  180.8 9.8 %all-to-all-start.5 = ((f32[8,1,64]{2,1,0:T(1,128)}), f32[8,1,64]{2,1,0:T(1,128)S(1)}, u32[]{:S(2)}, u32[]{:S(2)}) async-start(f32[8,1,64]{2,1,0:T(1,128)} %constant_dynamic-update-slice_fusion.8), calls=%async_computation.5 | async-start | bytes 8192 | tf_op jit(solution)/shard_map/all_to_all | solution.py:65
  190.6 9.7 %all-to-all-start.8 = ((f32[8,1,64]{2,1,0:T(1,128)}), f32[8,1,64]{2,1,0:T(1,128)S(1)}, u32[]{:S(2)}, u32[]{:S(2)}) async-start(f32[8,1,64]{2,1,0:T(1,128)} %constant_dynamic-update-slice_fusion.16), calls=%async_computation.8 | async-start | bytes 8192 | tf_op jit(solution)/shard_map/all_to_all | solution.py:65
  200.3 9.8 %all-to-all-start.7 = ((f32[1,8,64]{2,0,1:T(1,128)}), f32[1,8,64]{2,0,1:T(1,128)S(1)}, u32[]{:S(2)}, u32[]{:S(2)}) async-start(f32[1,8,64]{2,0,1:T(1,128)} %all_to_all.86), calls=%async_computation.7 | async-start | bytes 8192 | tf_op jit(solution)/shard_map/all_to_all | solution.py:63
  210.0 11.6 %all-to-all-start = ((f32[1,512,128]{2,0,1:T(1,128)}), f32[1,512,128]{2,0,1:T(1,128)S(1)}, u32[]{:S(2)}, u32[]{:S(2)}) async-start(f32[1,512,128]{2,0,1:T(1,128)} %bitcast.6), calls=%async_computation | async-start | bytes 524288 | tf_op jit(solution)/shard_map/all_to_all | solution.py:68
  221.6 38.8 %all-to-all-start.3 = ((f32[1,512,128]{2,0,1:T(1,128)}), f32[1,512,128]{2,0,1:T(1,128)S(1)}, u32[]{:S(2)}, u32[]{:S(2)}) async-start(f32[1,512,128]{2,0,1:T(1,128)} %bitcast.51), calls=%async_computation.3 | async-start | bytes 524288 | tf_op jit(solution)/shard_map/all_to_all | solution.py:68
  260.5 39.8 %all-to-all-start.6 = ((f32[1,512,128]{2,0,1:T(1,128)}), f32[1,512,128]{2,0,1:T(1,128)S(1)}, u32[]{:S(2)}, u32[]{:S(2)}) async-start(f32[1,512,128]{2,0,1:T(1,128)} %bitcast.96), calls=%async_computation.6 | async-start | bytes 524288 | tf_op jit(solution)/shard_map/all_to_all | solution.py:68
